TPU v7x, 32 devices: a whole 2x2x4 slice. The times are simulated.
32 devices in a mesh: outer: 8 (over z, x), inner: 4 (over y, core).
Axes of the slice: x: 2, y: 2, z: 4, core: 2. Of those that a mesh axis runs over, the one named last changes fastest.
Arguments:
- resid: bfloat16 [4096, 2048], P(('outer', 'inner')), may hold values from -40 to 40
- queries: bfloat16 [4096, 256], P(('outer', 'inner')), may hold values from -80 to 80
- keyvals: bfloat16 [4096, 256], P(('outer', 'inner')), may hold values from -10 to 10
- piece_order: int32 [8], replicated, may hold values from 0 to 7, each once
- out_proj: bfloat16 [256, 2048], replicated, may hold values from -0.75 to 0.75
- mlp_gain: float32 [2048], replicated, may hold values from 0.25 to 1.75
- w_gate: bfloat16 [2048, 7168], P('inner', 'outer'), may hold values from -0.125 to 0.125
- w_up: bfloat16 [2048, 7168], P('inner', 'outer'), may hold values from -0.125 to 0.125
- w_down: bfloat16 [7168, 2048], P('outer', 'inner'), may hold values from -0.0625 to 0.0625
Outputs:
- layer_out: bfloat16 [4096, 2048], P(('outer', 'inner'))
Inputs may be any that keep to these rules, and one draw needn't show every extreme that they name: `piece_order`: each of the 8 piece numbers appears once.
All inputs are finite; a program needn't handle non-finite values.
Results may differ from a plain program's by a relative error of at most 0.014.
Values may be sent and summed in bfloat16 or wider, within the bound.
A program may use at most 64 MiB of HBM per device.

v0:
```python
import jax
import jax.numpy as jnp
from jax import lax
from jax.sharding import PartitionSpec as P

HD = 128
QHEADS = 2


def passed_along(block, axis, distance):
    devices = range(lax.axis_size(axis))
    route = [(i - distance, i) for i in devices if i - distance in devices]
    return lax.ppermute(block, axis, route)


def attend(state_now, kv_part, visible, query_rows):
    running_max, running_sum, weighted = state_now
    key_rows = kv_part[:, :HD]
    value_rows = kv_part[:, HD:]
    scores = jnp.einsum(
        "rd,kd->rk", query_rows, key_rows, preferred_element_type=jnp.float32
    ) * HD ** (-0.5)
    scores = jnp.where(visible, scores, -1e30)
    new_max = jnp.maximum(running_max, jnp.max(scores, axis=1))
    weights = jnp.where(visible, jnp.exp(scores - new_max[:, None]), 0.0)
    factor = jnp.exp(running_max - new_max)
    running_sum = running_sum * factor + jnp.sum(weights, axis=1)
    weighted = weighted * factor[:, None] + jnp.dot(
        weights.astype(jnp.bfloat16), value_rows, preferred_element_type=jnp.float32
    )
    return (new_max, running_sum, weighted)


def per_device(resid, queries, keyvals, piece_order, out_proj, mlp_gain, w_gate, w_up, w_down):
    row_count = resid.shape[0]
    half_rows = row_count // 2
    gate_cols, up_cols, down_rows = (
        lax.all_gather(w_gate, "inner", axis=0, tiled=True),
        lax.all_gather(w_up, "inner", axis=0, tiled=True),
        lax.all_gather(w_down, "inner", axis=1, tiled=True),
    )
    block_pos = (
        piece_order[:, None] * half_rows + jnp.arange(half_rows, dtype=jnp.int32)[None, :]
    ).reshape(-1)
    query_pos = lax.dynamic_slice_in_dim(block_pos, lax.axis_index("inner") * row_count, row_count)
    row_pos = (query_pos[:, None] + jnp.zeros((1, QHEADS), jnp.int32)).reshape(-1)
    has_before = lax.axis_index("outer") > 0
    query_rows = queries.reshape(row_count * QHEADS, HD)
    before_kv = passed_along(keyvals, "outer", 1)
    total_rows = row_count * QHEADS
    start_state = (
        jnp.full((total_rows,), -1e30, jnp.float32),
        jnp.zeros((total_rows,), jnp.float32),
        jnp.zeros((total_rows, HD), jnp.float32),
    )
    state_now = start_state
    own_part = lax.all_gather(keyvals, "inner", axis=0, tiled=True)
    before_part = lax.all_gather(before_kv, "inner", axis=0, tiled=True)
    key_count = own_part.shape[0]
    own_visible = block_pos[None, :] <= row_pos[:, None]
    before_visible = jnp.broadcast_to(has_before, (row_pos.shape[0], key_count))
    state_now = attend(state_now, own_part, own_visible, query_rows)
    state_now = attend(state_now, before_part, before_visible, query_rows)
    running_max, running_sum, weighted = state_now
    attended = (
        (weighted / running_sum[:, None]).reshape(row_count, QHEADS * HD).astype(jnp.bfloat16)
    )
    after_attn = (
        resid.astype(jnp.float32) + jnp.dot(attended, out_proj, preferred_element_type=jnp.float32)
    ).astype(jnp.bfloat16)
    after_wide = after_attn.astype(jnp.float32)
    normed = (
        after_wide
        * lax.rsqrt(jnp.mean(after_wide * after_wide, axis=1, keepdims=True) + 1e-05)
        * mlp_gain
    ).astype(jnp.bfloat16)
    normed_part = lax.all_gather(normed, "outer", axis=0, tiled=True)
    gate = jnp.dot(normed_part, gate_cols, preferred_element_type=jnp.float32)
    upward = jnp.dot(normed_part, up_cols, preferred_element_type=jnp.float32)
    hidden = (jax.nn.silu(gate) * upward).astype(jnp.bfloat16)
    mlp_sum = lax.psum_scatter(
        jnp.dot(hidden, down_rows, preferred_element_type=jnp.float32).astype(jnp.bfloat16),
        "outer",
        scatter_dimension=0,
        tiled=True,
    ).astype(jnp.float32)
    return (after_wide + mlp_sum).astype(jnp.bfloat16)


def solution(mesh):
    placed = (
        P(("outer", "inner"), None),
        P(("outer", "inner"), None),
        P(("outer", "inner"), None),
        P(),
        P(),
        P(),
        P("inner", "outer"),
        P("inner", "outer"),
        P("outer", "inner"),
    )
    return jax.shard_map(
        per_device,
        mesh=mesh,
        in_specs=placed,
        out_specs=P(("outer", "inner"), None),
        check_vma=False,
    )
```

profile of v0, /device:TPU:0, one launch (start us, length us, event | category | flops | bytes accessed | tf_op | source)
XLA Modules:
  0.0 295.7 jit_solution(5640980260196293325)
XLA Ops:
  6.5 0.7 all-gather.7.cloned.1.call-update
  7.3 4.9 %collective-permute-start = (bf16[128,256]{1,0:T(8,128)(2,1)}, bf16[128,256]{1,0:T(8,128)(2,1)S(1)}, u32[]{:S(2)}, u32[]{:S(2)}) collective-permute-start(bf16[128,256]{1,0:T(8,128)(2,1)} %param.11), channel_id=1, source_target_pairs={{0,4},{4,8},{8,12},{12,16},{16,20},{20,24},{24,28},{1,5},{5,9},{9,... | collective-permute-start | bytes 196616 | tf_op jit(solution)/shard_map/ppermute | solution.py:13
  12.2 0.7 broadcast_multiply_fusion
  13.2 0.2 le.16
  13.3 0.9 reshape.65
  14.2 6.0 %all_gather.18 = bf16[512,256]{1,0:T(8,128)(2,1)S(1)} all-gather(bf16[128,256]{1,0:T(8,128)(2,1)} %param.11), channel_id=1, replica_groups=mesh['outer'=8,'inner'=4] {'inner'}, dimensions={0}, use_global_device_ids=true | all-gather | bytes 327680 | tf_op jit(solution)/shard_map/all_gather | solution.py:57
  20.2 0.3 fusion.28
  20.5 7.7 %all_gather.19 = bf16[512,256]{1,0:T(8,128)(2,1)S(1)} all-gather(bf16[128,256]{1,0:T(8,128)(2,1)S(1)} %collective-permute-done), channel_id=1, replica_groups=mesh['outer'=8,'inner'=4] {'inner'}, dimensions={0}, use_global_device_ids=true | all-gather | bytes 327680 | tf_op jit(solution)/shard_map/all_gather | solution.py:58
  28.2 0.3 fusion.29
  28.5 0.4 fusion.7
  28.9 0.3 fusion.5
  29.2 0.3 fusion.6
  29.6 0.4 multiply_reduce_fusion
  30.0 1.0 multiply_convert_fusion.1
  31.0 0.7 all-gather.9.cloned.1.call-update
  31.8 0.5 all-gather.11.cloned.1.call-update
  32.3 12.2 %all-gather.7.cloned.1.call-done = bf16[2048,896]{1,0:T(8,128)(2,1)} async-done(((bf16[512,896]{1,0:T(8,128)(2,1)}), bf16[2048,896]{1,0:T(8,128)(2,1)}) %all-gather.7.cloned.1.call-update) | async-done | bytes 3670032 | tf_op jit(solution)/shard_map/all_gather | solution.py:38
  44.5 74.9 %all-gather.5.cloned.1.call-done = bf16[1024,2048]{1,0:T(8,128)(2,1)} async-done(((bf16[128,2048]{1,0:T(8,128)(2,1)}), bf16[1024,2048]{1,0:T(8,128)(2,1)}) %all-gather.5.cloned.1.call-update) | async-done | bytes 4194320 | tf_op jit(solution)/shard_map/all_gather | solution.py:77
  119.5 9.6 %fusion.30 = f32[1024,896]{1,0:T(8,128)} fusion(bf16[1024,2048]{1,0:T(8,128)(2,1)} %all-gather.5.cloned.1.call-done, bf16[2048,896]{1,0:T(8,128)(2,1)} %all-gather.7.cloned.1.call-done), kind=kOutput, calls=%fused_computation.47 | convolution fusion | flops 3758096384 | bytes 11534336 | tf_op jit(solution)/shard_map/dot_general | solution.py:78
  129.1 22.0 %all-gather.9.cloned.1.call-done = bf16[2048,896]{1,0:T(8,128)(2,1)} async-done(((bf16[512,896]{1,0:T(8,128)(2,1)}), bf16[2048,896]{1,0:T(8,128)(2,1)}) %all-gather.9.cloned.1.call-update) | async-done | bytes 3670032 | tf_op jit(solution)/shard_map/all_gather | solution.py:39
  151.1 32.9 %all-gather.11.cloned.1.call-done = bf16[896,2048]{1,0:T(8,128)(2,1)} async-done(((bf16[896,512]{1,0:T(8,128)(2,1)}), bf16[896,2048]{1,0:T(8,128)(2,1)}) %all-gather.11.cloned.1.call-update) | async-done | bytes 3670032 | tf_op jit(solution)/shard_map/all_gather | solution.py:40
  184.0 14.7 %convolution_convert_fusion = bf16[1024,2048]{1,0:T(8,128)(2,1)} fusion(bf16[896,2048]{1,0:T(8,128)(2,1)} %all-gather.11.cloned.1.call-done, f32[1024,896]{1,0:T(8,128)} %fusion.30, bf16[1024,2048]{1,0:T(8,128)(2,1)} %all-gather.5.cloned.1.call-done, bf16[2048,896]{1,0:T(8,128)(2,1)} %all-gather.9.cloned.1.call-done), kind=kOutput, calls=%fused_computation | convolution fusion | flops 7523794944 | bytes 19398656 | tf_op jit(solution)/shard_map/dot_general | solution.py:82
  198.8 88.5 %reduce-scatter.2.cloned.1.call-done = bf16[128,2048]{1,0:T(8,128)(2,1)} async-done(((bf16[1024,2048]{1,0:T(8,128)(2,1)}), bf16[128,2048]{1,0:T(8,128)(2,1)}) %reduce-scatter.2.cloned.1.call-update) | async-done | bytes 524304 | tf_op jit(solution)/shard_map/reduce_scatter | solution.py:81
  287.3 1.9 add_convert_fusion
  (22 shorter events, 0.6 us)
Async XLA Ops:
  6.5 23.0 %copy-start = (bf16[256,2048]{1,0:T(8,128)(2,1)S(1)}, bf16[256,2048]{1,0:T(8,128)(2,1)}, u32[]{:S(2)}) copy-start(bf16[256,2048]{1,0:T(8,128)(2,1)} %param.13) | copy-start | bytes 3145732
  6.5 23.0 %copy-start.1 = (bf16[128,2048]{1,0:T(8,128)(2,1)S(1)}, bf16[128,2048]{1,0:T(8,128)(2,1)}, u32[]{:S(2)}) copy-start(bf16[128,2048]{1,0:T(8,128)(2,1)} %param.9) | copy-start | bytes 1572868
  6.5 38.0 %all-gather.7.cloned.1.call-start = ((), (), s32[]{:S(2)}) async-start(), calls=%async_computation.2 | async-start | bytes 4587520 | tf_op jit(solution)/shard_map/all_gather | solution.py:38
  7.3 112.2 %all-gather.5.cloned.1.call-start = ((), (), s32[]{:S(2)}) async-start(), calls=%async_computation.1 | async-start | bytes 4718592 | tf_op jit(solution)/shard_map/all_gather | solution.py:77
  7.3 13.2 %collective-permute-start = (bf16[128,256]{1,0:T(8,128)(2,1)}, bf16[128,256]{1,0:T(8,128)(2,1)S(1)}, u32[]{:S(2)}, u32[]{:S(2)}) collective-permute-start(bf16[128,256]{1,0:T(8,128)(2,1)} %param.11), channel_id=1, source_target_pairs={{0,4},{4,8},{8,12},{12,16},{16,20},{20,24},{24,28},{1,5},{5,9},{9,... | collective-permute-start | bytes 196616 | tf_op jit(solution)/shard_map/ppermute | solution.py:13
  20.5 9.5 %copy-start.2 = (f32[2048]{0:T(1024)S(1)}, f32[2048]{0:T(1024)}, u32[]{:S(2)}) copy-start(f32[2048]{0:T(1024)} %param.14) | copy-start | bytes 24580
  31.0 120.1 %all-gather.9.cloned.1.call-start = ((), (), s32[]{:S(2)}) async-start(), calls=%async_computation.3 | async-start | bytes 4587520 | tf_op jit(solution)/shard_map/all_gather | solution.py:39
  31.7 152.3 %all-gather.11.cloned.1.call-start = ((), (), s32[]{:S(2)}) async-start(), calls=%async_computation.4 | async-start | bytes 4587520 | tf_op jit(solution)/shard_map/all_gather | solution.py:40
  32.3 255.0 %reduce-scatter.2.cloned.1.call-start = ((), (), s32[]{:S(2)}) async-start(), calls=%async_computation.5 | async-start | bytes 4718592 | tf_op jit(solution)/shard_map/reduce_scatter | solution.py:81
Sparse Core Ops, SparseCore 0:
  8.9 35.6 all-gather.6
  46.7 72.7 all-gather.4
  121.1 30.0 all-gather.8
  152.5 31.4 all-gather.10
  198.9 88.3 reduce-scatter.1
where the time goes:
time: 296 us
  waiting for transfers between devices  232 us (78%)
  matrix products  26 us (9%)
  blocking collectives  13.7 us (5%)
  between operations  13.2 us (4%)
  starting transfers between devices  5.03 us (2%)
  other arithmetic  4.03 us (1%)
    reduce_scatter x1, waiting for transfers between devices, per_device(): lax.psum_scatter(jnp.dot(hidden, down_rows, preferred_element_type=jnp.fl...  88.5 us
    all_gather x1, waiting for transfers between devices, per_device(): normed_part = lax.all_gather(normed, 'outer', axis=0, tiled=True)  74.9 us
    all_gather x1, waiting for transfers between devices, per_device(): lax.all_gather(w_down, 'inner', axis=1, tiled=True)  32.9 us
    all_gather x1, waiting for transfers between devices, per_device(): lax.all_gather(w_up, 'inner', axis=0, tiled=True)  22 us
    dot_general x1, matrix products, per_device(): jnp.dot(hidden, down_rows, preferred_element_type=jnp.float32)  14.7 us
    all_gather x1, waiting for transfers between devices, per_device(): lax.all_gather(w_gate, 'inner', axis=0, tiled=True)  12.2 us
    dot_general x1, matrix products, per_device(): gate = jnp.dot(normed_part, gate_cols, preferred_element_type=jnp.float32)  9.63 us
    all_gather x1, blocking collectives, per_device(): before_part = lax.all_gather(before_kv, 'inner', axis=0, tiled=True)  7.72 us
  transfers between devices with their start and end apart: 6, of which 5 were waited for; matrix products, arithmetic and copies ran while one was open for 5% of the time, Pallas kernels for 0%

commit v1 on v0

--- a/solution.py
+++ b/solution.py
@@ -74,7 +74,14 @@
         * lax.rsqrt(jnp.mean(after_wide * after_wide, axis=1, keepdims=True) + 1e-05)
         * mlp_gain
     ).astype(jnp.bfloat16)
-    normed_part = lax.all_gather(normed, "outer", axis=0, tiled=True)
+    ring = [normed]
+    for hop in range(7):
+        ring.append(lax.ppermute(ring[-1], "outer", [(dev, (dev + 1) % 8) for dev in range(8)]))
+    normed_part = jnp.roll(
+        jnp.concatenate(ring[::-1], axis=0),
+        (lax.axis_index("outer") + 1) * ring[0].shape[0],
+        axis=0,
+    )
     gate = jnp.dot(normed_part, gate_cols, preferred_element_type=jnp.float32)
     upward = jnp.dot(normed_part, up_cols, preferred_element_type=jnp.float32)
     hidden = (jax.nn.silu(gate) * upward).astype(jnp.bfloat16)

time: 296 us -> 275 us (0.929)
  waiting for transfers between devices: 232 us -> 186 us
  local copies, waits for them, and re-layouts: 1.29 us -> 22.9 us
    ppermute x0 -> x7, waiting for transfers between devices: none -> 99 us  [per_device(): lax.ppermute(ring[-1], 'outer', [(dev, (dev + 1) % 8) for dev in range(8)])]
    all_gather x1 -> x0, waiting for transfers between devices: 74.9 us -> none  [per_device(): normed_part = lax.all_gather(normed, 'outer', axis=0, tiled=True)]
    all_gather x1, waiting for transfers between devices: 32.9 us -> 0.01 us  [per_device(): lax.all_gather(w_down, 'inner', axis=1, tiled=True)]
    all_gather x1, waiting for transfers between devices: 22 us -> 0.01 us  [per_device(): lax.all_gather(w_up, 'inner', axis=0, tiled=True)]
    unnamed x6 -> x30, local copies, waits for them, and re-layouts: 0.01 us -> 21.6 us
    all_gather x1, waiting for transfers between devices: 12.2 us -> 0.01 us  [per_device(): lax.all_gather(w_gate, 'inner', axis=0, tiled=True)]
  transfers between devices with their start and end apart: 6 -> 12, of which waited for: 5 -> 8; matrix products, arithmetic and copies ran while one was open for 5% -> 13% of each run, Pallas kernels for 0% -> 0%
where the time goes in v1:
time: 275 us; the launch traced here: 274 us
  waiting for transfers between devices  186 us (68%)
  matrix products  27.1 us (10%)
  local copies, waits for them, and re-layouts  22.9 us (8%)
  blocking collectives  13.7 us (5%)
  between operations  13.3 us (5%)
  starting transfers between devices  6.64 us (2%)
  other arithmetic  5.2 us (2%)
    ppermute x7, waiting for transfers between devices, per_device(): lax.ppermute(ring[-1], 'outer', [(dev, (dev + 1) % 8) for dev in range(8)])  99 us
    reduce_scatter x1, waiting for transfers between devices, per_device(): lax.psum_scatter(jnp.dot(hidden, down_rows, preferred_element_type=jnp.fl...  85.8 us
    unnamed x30, local copies, waits for them, and re-layouts  21.6 us
    dot_general x1, matrix products, per_device(): jnp.dot(hidden, down_rows, preferred_element_type=jnp.float32)  14.8 us
    dot_general x1, matrix products, per_device(): upward = jnp.dot(normed_part, up_cols, preferred_element_type=jnp.float32)  9.66 us
    all_gather x1, blocking collectives, per_device(): before_part = lax.all_gather(before_kv, 'inner', axis=0, tiled=True)  7.71 us
    all_gather x1, blocking collectives, per_device(): own_part = lax.all_gather(keyvals, 'inner', axis=0, tiled=True)  5.99 us
  transfers between devices with their start and end apart: 12, of which 8 were waited for; matrix products, arithmetic and copies ran while one was open for 13% of the time, Pallas kernels for 0%

profile of v1, /device:TPU:0, one launch (start us, length us, event | category | flops | bytes accessed | tf_op | source)
XLA Modules:
  0.0 274.4 jit_solution(17876393473443235859)
XLA Ops:
  7.3 4.9 %collective-permute-start = (bf16[128,256]{1,0:T(8,128)(2,1)}, bf16[128,256]{1,0:T(8,128)(2,1)S(1)}, u32[]{:S(2)}, u32[]{:S(2)}) collective-permute-start(bf16[128,256]{1,0:T(8,128)(2,1)} %param.11), channel_id=1, source_target_pairs={{0,4},{4,8},{8,12},{12,16},{16,20},{20,24},{24,28},{1,5},{5,9},{9,... | collective-permute-start | bytes 196616 | tf_op jit(solution)/shard_map/ppermute | solution.py:13
  12.3 6.0 %all_gather.15 = bf16[512,256]{1,0:T(8,128)(2,1)S(1)} all-gather(bf16[128,256]{1,0:T(8,128)(2,1)} %param.11), channel_id=1, replica_groups=mesh['outer'=8,'inner'=4] {'inner'}, dimensions={0}, use_global_device_ids=true | all-gather | bytes 327680 | tf_op jit(solution)/shard_map/all_gather | solution.py:57
  20.6 7.7 %all_gather.16 = bf16[512,256]{1,0:T(8,128)(2,1)S(1)} all-gather(bf16[128,256]{1,0:T(8,128)(2,1)S(1)} %collective-permute-done), channel_id=1, replica_groups=mesh['outer'=8,'inner'=4] {'inner'}, dimensions={0}, use_global_device_ids=true | all-gather | bytes 327680 | tf_op jit(solution)/shard_map/all_gather | solution.py:58
  29.6 1.4 multiply_reduce_fusion
  31.2 1.6 collective-permute-start.1
  32.9 15.3 %collective-permute-done.1 = bf16[128,2048]{1,0:T(8,128)(2,1)S(1)} collective-permute-done((bf16[128,2048]{1,0:T(8,128)(2,1)S(1)}, bf16[128,2048]{1,0:T(8,128)(2,1)S(1)}, u32[]{:S(2)}, u32[]{:S(2)}) %collective-permute-start.1) | collective-permute-done | bytes 524320 | tf_op jit(solution)/shard_map/ppermute | solution.py:79
  48.2 16.0 %collective-permute-done.2 = bf16[128,2048]{1,0:T(8,128)(2,1)S(1)} collective-permute-done((bf16[128,2048]{1,0:T(8,128)(2,1)S(1)}, bf16[128,2048]{1,0:T(8,128)(2,1)S(1)}, u32[]{:S(2)}, u32[]{:S(2)}) %collective-permute-start.2) | collective-permute-done | bytes 524320 | tf_op jit(solution)/shard_map/ppermute | solution.py:79
  64.2 15.2 %collective-permute-done.3 = bf16[128,2048]{1,0:T(8,128)(2,1)S(1)} collective-permute-done((bf16[128,2048]{1,0:T(8,128)(2,1)S(1)}, bf16[128,2048]{1,0:T(8,128)(2,1)S(1)}, u32[]{:S(2)}, u32[]{:S(2)}) %collective-permute-start.3) | collective-permute-done | bytes 524320 | tf_op jit(solution)/shard_map/ppermute | solution.py:79
  80.1 14.3 %collective-permute-done.4 = bf16[128,2048]{1,0:T(8,128)(2,1)S(1)} collective-permute-done((bf16[128,2048]{1,0:T(8,128)(2,1)S(1)}, bf16[128,2048]{1,0:T(8,128)(2,1)S(1)}, u32[]{:S(2)}, u32[]{:S(2)}) %collective-permute-start.4) | collective-permute-done | bytes 524320 | tf_op jit(solution)/shard_map/ppermute | solution.py:79
  95.3 13.4 %collective-permute-done.5 = bf16[128,2048]{1,0:T(8,128)(2,1)S(1)} collective-permute-done((bf16[128,2048]{1,0:T(8,128)(2,1)S(1)}, bf16[128,2048]{1,0:T(8,128)(2,1)S(1)}, u32[]{:S(2)}, u32[]{:S(2)}) %collective-permute-start.5) | collective-permute-done | bytes 524320 | tf_op jit(solution)/shard_map/ppermute | solution.py:79
  109.5 12.7 %collective-permute-done.6 = bf16[128,2048]{1,0:T(8,128)(2,1)} collective-permute-done((bf16[128,2048]{1,0:T(8,128)(2,1)S(1)}, bf16[128,2048]{1,0:T(8,128)(2,1)}, u32[]{:S(2)}, u32[]{:S(2)}) %collective-permute-start.6) | collective-permute-done | bytes 524320 | tf_op jit(solution)/shard_map/ppermute | solution.py:79
  122.3 12.1 %collective-permute-done.7 = bf16[128,2048]{1,0:T(8,128)(2,1)} collective-permute-done((bf16[128,2048]{1,0:T(8,128)(2,1)}, bf16[128,2048]{1,0:T(8,128)(2,1)}, u32[]{:S(2)}, u32[]{:S(2)}) %collective-permute-start.7) | collective-permute-done | bytes 524320 | tf_op jit(solution)/shard_map/ppermute | solution.py:79
  134.4 1.9 constant_dynamic-update-slice_fusion.15
  136.3 1.9 constant_dynamic-update-slice_fusion.14
  138.2 1.9 constant_dynamic-update-slice_fusion.13
  140.1 1.9 constant_dynamic-update-slice_fusion.12
  142.0 1.9 constant_dynamic-update-slice_fusion.11
  146.5 1.9 constant_dynamic-update-slice_fusion.7
  148.4 1.9 constant_dynamic-update-slice_fusion.6
  154.6 1.0 constant_dynamic-update-slice_fusion
  155.6 9.7 %fusion = f32[1024,896]{1,0:T(8,128)} fusion(bf16[2048,896]{1,0:T(8,128)(2,1)} %all-gather.6.cloned.1.call-done, bf16[2048,2048]{1,0:T(8,128)(2,1)} %constant_dynamic-update-slice_fusion, s32[]{:T(128)S(6)} %select_n.35), kind=kOutput, calls=%fused_computation.1 | convolution fusion | flops 3758096384 | bytes 11534340 | tf_op jit(solution)/shard_map/dot_general | solution.py:86
  165.3 14.8 %convolution_convert_fusion = bf16[1024,2048]{1,0:T(8,128)(2,1)} fusion(bf16[896,2048]{1,0:T(8,128)(2,1)} %all-gather.8.cloned.1.call-done, f32[1024,896]{1,0:T(8,128)} %fusion, bf16[2048,896]{1,0:T(8,128)(2,1)} %all-gather.4.cloned.1.call-done, bf16[2048,2048]{1,0:T(8,128)(2,1)} %constant_dynamic-update-slice_fusion, s32[]{:T(128)S(6)} %select_n.35), kind=kOutput, calls=%fused_computation | convolution fusion | flops 7523794944 | bytes 19398660 | tf_op jit(solution)/shard_map/dot_general | solution.py:89
  180.1 85.8 %reduce-scatter.2.cloned.1.call-done = bf16[128,2048]{1,0:T(8,128)(2,1)} async-done(((bf16[1024,2048]{1,0:T(8,128)(2,1)}), bf16[128,2048]{1,0:T(8,128)(2,1)}) %reduce-scatter.2.cloned.1.call-update) | async-done | bytes 524304 | tf_op jit(solution)/shard_map/reduce_scatter | solution.py:88
  266.0 1.9 add_convert_fusion
  (59 shorter events, 14.0 us)
Async XLA Ops:
  6.5 23.1 %copy-start = (bf16[256,2048]{1,0:T(8,128)(2,1)S(1)}, bf16[256,2048]{1,0:T(8,128)(2,1)}, u32[]{:S(2)}) copy-start(bf16[256,2048]{1,0:T(8,128)(2,1)} %param.13) | copy-start | bytes 3145732
  6.5 24.5 %copy-start.7 = (f32[2048]{0:T(1024)S(1)}, f32[2048]{0:T(1024)}, u32[]{:S(2)}) copy-start(f32[2048]{0:T(1024)} %param.14) | copy-start | bytes 24580
  6.5 149.0 %all-gather.6.cloned.1.call-start = ((), (), s32[]{:S(2)}) async-start(), calls=%async_computation.2 | async-start | bytes 4587520 | tf_op jit(solution)/shard_map/all_gather | solution.py:39
  7.3 158.0 %all-gather.4.cloned.1.call-start = ((), (), s32[]{:S(2)}) async-start(), calls=%async_computation.1 | async-start | bytes 4587520 | tf_op jit(solution)/shard_map/all_gather | solution.py:38
  7.3 13.3 %collective-permute-start = (bf16[128,256]{1,0:T(8,128)(2,1)}, bf16[128,256]{1,0:T(8,128)(2,1)S(1)}, u32[]{:S(2)}, u32[]{:S(2)}) collective-permute-start(bf16[128,256]{1,0:T(8,128)(2,1)} %param.11), channel_id=1, source_target_pairs={{0,4},{4,8},{8,12},{12,16},{16,20},{20,24},{24,28},{1,5},{5,9},{9,... | collective-permute-start | bytes 196616 | tf_op jit(solution)/shard_map/ppermute | solution.py:13
  12.2 153.0 %all-gather.8.cloned.1.call-start = ((), (), s32[]{:S(2)}) async-start(), calls=%async_computation.3 | async-start | bytes 4587520 | tf_op jit(solution)/shard_map/all_gather | solution.py:40
  31.2 16.9 %collective-permute-start.1 = (bf16[128,2048]{1,0:T(8,128)(2,1)S(1)}, bf16[128,2048]{1,0:T(8,128)(2,1)S(1)}, u32[]{:S(2)}, u32[]{:S(2)}) collective-permute-start(bf16[128,2048]{1,0:T(8,128)(2,1)S(1)} %multiply_convert_fusion.2), channel_id=1, source_target_pairs={{0,4},{4,8},{8,12},{12,16},{16,20},{20,24},{24,28},{28,0},{1,5},{5... | collective-permute-start | bytes 1572872 | tf_op jit(solution)/shard_map/ppermute | solution.py:79
  48.2 16.0 %collective-permute-start.2 = (bf16[128,2048]{1,0:T(8,128)(2,1)S(1)}, bf16[128,2048]{1,0:T(8,128)(2,1)S(1)}, u32[]{:S(2)}, u32[]{:S(2)}) collective-permute-start(bf16[128,2048]{1,0:T(8,128)(2,1)S(1)} %collective-permute-done.1), channel_id=1, source_target_pairs={{0,4},{4,8},{8,12},{12,16},{16,20},{20,24},{24,28},{28,0},{1,5},{5... | collective-permute-start | bytes 1572872 | tf_op jit(solution)/shard_map/ppermute | solution.py:79
  64.2 15.2 %collective-permute-start.3 = (bf16[128,2048]{1,0:T(8,128)(2,1)S(1)}, bf16[128,2048]{1,0:T(8,128)(2,1)S(1)}, u32[]{:S(2)}, u32[]{:S(2)}) collective-permute-start(bf16[128,2048]{1,0:T(8,128)(2,1)S(1)} %collective-permute-done.2), channel_id=1, source_target_pairs={{0,4},{4,8},{8,12},{12,16},{16,20},{20,24},{24,28},{28,0},{1,5},{5... | collective-permute-start | bytes 1572872 | tf_op jit(solution)/shard_map/ppermute | solution.py:79
  79.3 0.8 copy-start.1
  80.1 14.3 %collective-permute-start.4 = (bf16[128,2048]{1,0:T(8,128)(2,1)S(1)}, bf16[128,2048]{1,0:T(8,128)(2,1)S(1)}, u32[]{:S(2)}, u32[]{:S(2)}) collective-permute-start(bf16[128,2048]{1,0:T(8,128)(2,1)S(1)} %collective-permute-done.3), channel_id=1, source_target_pairs={{0,4},{4,8},{8,12},{12,16},{16,20},{20,24},{24,28},{28,0},{1,5},{5... | collective-permute-start | bytes 1572872 | tf_op jit(solution)/shard_map/ppermute | solution.py:79
  94.5 0.8 copy-start.3
  95.2 13.4 %collective-permute-start.5 = (bf16[128,2048]{1,0:T(8,128)(2,1)S(1)}, bf16[128,2048]{1,0:T(8,128)(2,1)S(1)}, u32[]{:S(2)}, u32[]{:S(2)}) collective-permute-start(bf16[128,2048]{1,0:T(8,128)(2,1)S(1)} %collective-permute-done.4), channel_id=1, source_target_pairs={{0,4},{4,8},{8,12},{12,16},{16,20},{20,24},{24,28},{28,0},{1,5},{5... | collective-permute-start | bytes 1572872 | tf_op jit(solution)/shard_map/ppermute | solution.py:79
  108.7 0.8 copy-start.5
  109.5 12.7 %collective-permute-start.6 = (bf16[128,2048]{1,0:T(8,128)(2,1)S(1)}, bf16[128,2048]{1,0:T(8,128)(2,1)}, u32[]{:S(2)}, u32[]{:S(2)}) collective-permute-start(bf16[128,2048]{1,0:T(8,128)(2,1)S(1)} %collective-permute-done.5), channel_id=1, source_target_pairs={{0,4},{4,8},{8,12},{12,16},{16,20},{20,24},{24,28},{28,0},{1,5},{5... | collective-permute-start | bytes 1572872 | tf_op jit(solution)/shard_map/ppermute | solution.py:79
  122.2 12.2 %collective-permute-start.7 = (bf16[128,2048]{1,0:T(8,128)(2,1)}, bf16[128,2048]{1,0:T(8,128)(2,1)}, u32[]{:S(2)}, u32[]{:S(2)}) collective-permute-start(bf16[128,2048]{1,0:T(8,128)(2,1)} %collective-permute-done.6), channel_id=1, source_target_pairs={{0,4},{4,8},{8,12},{12,16},{16,20},{20,24},{24,28},{28,0},{1,5},{5... | collective-permute-start | bytes 1572872 | tf_op jit(solution)/shard_map/ppermute | solution.py:79
  122.2 143.7 %reduce-scatter.2.cloned.1.call-start = ((), (), s32[]{:S(2)}) async-start(), calls=%async_computation.4 | async-start | bytes 4718592 | tf_op jit(solution)/shard_map/reduce_scatter | solution.py:88
  122.3 28.0 %copy-start.6 = (bf16[128,2048]{1,0:T(8,128)(2,1)S(1)}, bf16[128,2048]{1,0:T(8,128)(2,1)}, u32[]{:S(2)}) copy-start(bf16[128,2048]{1,0:T(8,128)(2,1)} %copy-done.5) | copy-start | bytes 1572868
  122.3 28.9 %copy-start.4 = (bf16[128,2048]{1,0:T(8,128)(2,1)S(1)}, bf16[128,2048]{1,0:T(8,128)(2,1)}, u32[]{:S(2)}) copy-start(bf16[128,2048]{1,0:T(8,128)(2,1)} %copy-done.3) | copy-start | bytes 1572868
  122.3 29.8 %copy-start.2 = (bf16[128,2048]{1,0:T(8,128)(2,1)S(1)}, bf16[128,2048]{1,0:T(8,128)(2,1)}, u32[]{:S(2)}) copy-start(bf16[128,2048]{1,0:T(8,128)(2,1)} %copy-done.1) | copy-start | bytes 1572868
Sparse Core Ops, SparseCore 0:
  8.9 35.6 all-gather.5
  46.1 31.4 all-gather.3
  122.3 32.9 all-gather.7
  180.2 85.6 reduce-scatter.1
